TPU v7x, 32 devices: a whole 2x2x4 slice. The times are simulated.
32 devices in a mesh: row: 8 (over z, x), col: 4 (over y, core).
Axes of the slice: x: 2, y: 2, z: 4, core: 2. Of those that a mesh axis runs over, the one named last changes fastest.
Arguments:
- momentum: bfloat16 [16384, 16384], P('row', 'col'), may hold values from -16 to 16
- gradient: bfloat16 [16384, 16384], P('row', 'col'), may hold values from -6 to 6
- right_basis: bfloat16 [1024, 16384], P('row', 'col'), may hold values from -1 to 1
Outputs:
- momentum_next: bfloat16 [16384, 16384], P('row', 'col')
- basis_next: float32 [1024, 16384], P('row', 'col')
- update: bfloat16 [16384, 16384], P('row', 'col')
All inputs are finite; a program needn't handle non-finite values.
Results may differ from a plain program's by a relative error of at most 0.02.
Values may be sent and summed in bfloat16 or wider, within the bound.
A program may use at most 128 MiB of HBM per device.

v0:
```python
import math
import jax
import jax.numpy as jnp
from jax import lax
from jax.sharding import PartitionSpec as P

D = 16384
RANK = 1024
momentum_decay = 0.95
epsilon = 1e-06


def orthonormalize(projected, gram_matrix):
    lower_factor = jnp.linalg.cholesky(gram_matrix)
    solved = jax.scipy.linalg.solve_triangular(lower_factor, projected.T, lower=True)
    return solved.T.astype(jnp.bfloat16)


def self_gram(projected):
    return lax.dot_general(
        projected, projected, (((0,), (0,)), ((), ())), precision=lax.Precision.HIGHEST
    )


def body(momentum, gradient, right_basis):
    buffer = (momentum.astype(jnp.float32) + gradient.astype(jnp.float32)).astype(jnp.bfloat16)
    rank_rows = right_basis.shape[0]
    partial_value = lax.dot_general(
        buffer,
        lax.all_gather(right_basis, "row", axis=0, tiled=True),
        (((1,), (1,)), ((), ())),
        preferred_element_type=jnp.float32,
    )
    row_share = lax.psum_scatter(
        partial_value.astype(jnp.bfloat16), "col", scatter_dimension=0, tiled=True
    ).astype(jnp.float32)
    gram_matrix = lax.psum(self_gram(row_share), ("row", "col"))
    ortho_share = orthonormalize(row_share, gram_matrix)
    orthonormal = lax.all_gather(ortho_share, "col", axis=0, tiled=True)
    right_share = lax.psum_scatter(
        lax.dot_general(
            orthonormal, buffer, (((0,), (0,)), ((), ())), preferred_element_type=jnp.float32
        ).astype(jnp.bfloat16),
        "row",
        scatter_dimension=0,
        tiled=True,
    )
    right_wide = right_share.astype(jnp.float32)
    gathered = lax.all_gather(right_share, "row", axis=0, tiled=True)
    gathered_wide = gathered.astype(jnp.float32)
    sums_total = lax.psum(jnp.sum(gathered_wide * gathered_wide, axis=1), "col")
    inverse_norm = lax.rsqrt(sums_total + epsilon)[:, None]
    scaled = (gathered_wide * inverse_norm).astype(jnp.bfloat16)
    feedback = jnp.dot(orthonormal, gathered, preferred_element_type=jnp.float32)
    direction = jnp.dot(orthonormal, scaled, preferred_element_type=jnp.float32)
    offset = lax.axis_index("row") * rank_rows
    basis_next = right_wide * lax.dynamic_slice_in_dim(inverse_norm, offset, rank_rows, 0)
    momentum_next = (buffer.astype(jnp.float32) - (1.0 - momentum_decay) * feedback).astype(
        jnp.bfloat16
    )
    update_scale = D / math.sqrt(RANK)
    update = (update_scale * direction).astype(jnp.bfloat16)
    return (momentum_next, basis_next, update)


def solution(mesh):
    return jax.shard_map(
        body,
        mesh=mesh,
        in_specs=(P("row", "col"), P("row", "col"), P("row", "col")),
        out_specs=(P("row", "col"), P("row", "col"), P("row", "col")),
        check_vma=False,
    )
```

profile of v0, /device:TPU:0, one launch (start us, length us, event | category | flops | bytes accessed | tf_op | source)
XLA Modules:
  0.0 1132.3 jit_solution(6209591932826324028)
XLA Ops:
  7.9 129.4 %all-gather.4.cloned.1.call-done = bf16[1024,4096]{1,0:T(8,128)(2,1)} async-done(((bf16[128,4096]{1,0:T(8,128)(2,1)}), bf16[1024,4096]{1,0:T(8,128)(2,1)}) %all-gather.4.cloned.1.call-update) | async-done | bytes 8388624 | tf_op jit(solution)/shard_map/all_gather | solution.py:30
  137.3 25.8 %convolution_convert_fusion.1 = bf16[2048,1024]{1,0:T(8,128)(2,1)} fusion(bf16[1024,4096]{1,0:T(8,128)(2,1)} %all-gather.4.cloned.1.call-done, bf16[2048,4096]{1,0:T(8,128)(2,1)} %param.4, bf16[2048,4096]{1,0:T(8,128)(2,1)} %param.3), kind=kOutput, calls=%fused_computation.15 | convolution fusion | flops 17215520768 | bytes 46137344 | tf_op jit(solution)/shard_map/dot_general | solution.py:28
  163.2 42.9 %reduce-scatter.3.cloned.1.call-done = bf16[512,1024]{1,0:T(8,128)(2,1)} async-done(((bf16[2048,1024]{1,0:T(8,128)(2,1)}), bf16[512,1024]{1,0:T(8,128)(2,1)}) %reduce-scatter.3.cloned.1.call-update) | async-done | bytes 1048592 | tf_op jit(solution)/shard_map/reduce_scatter | solution.py:34
  206.1 4.9 fusion.67
  211.3 143.2 %all-reduce.3.cloned.1.call-done = f32[1024,1024]{0,1:T(8,128)} async-done(((f32[1024,1024]{0,1:T(8,128)}), f32[1024,1024]{0,1:T(8,128)}) %all-reduce.3.cloned.1.call-update) | async-done | bytes 4194320 | tf_op jit(solution)/shard_map/psum | solution.py:37
  354.5 5.5 copy.7
  360.0 4.4 fusion.4
  366.5 11.7 %cholesky.223 = f32[128,128]{1,0:T(8,128)S(1)} custom-call(f32[128,128]{1,0:T(8,128)S(1)} %cholesky.580), custom_call_target="Cholesky" | custom-call | tf_op jit(solution)/shard_map/jit(cholesky)/cholesky | solution.py:14
  378.2 9.8 custom-call.63
  388.1 2.5 cholesky.255
  395.2 12.1 %cholesky.244 = f32[128,128]{1,0:T(8,128)S(1)} custom-call(f32[128,128]{1,0:T(8,128)S(1)} %cholesky.584), custom_call_target="Cholesky" | custom-call | tf_op jit(solution)/shard_map/jit(cholesky)/cholesky | solution.py:14
  408.0 9.8 custom-call.64
  422.7 13.2 %cholesky.468 = f32[128,128]{1,0:T(8,128)} custom-call(f32[128,128]{1,0:T(8,128)} %cholesky.589), custom_call_target="Cholesky" | custom-call | tf_op jit(solution)/shard_map/jit(cholesky)/cholesky | solution.py:14
  438.0 11.3 custom-call.65
  451.2 2.3 convolution_subtract_fusion.2
  453.6 12.5 %cholesky.487 = f32[128,128]{1,0:T(8,128)} custom-call(f32[128,128]{1,0:T(8,128)S(1)} %cholesky.594), custom_call_target="Cholesky" | custom-call | tf_op jit(solution)/shard_map/jit(cholesky)/cholesky | solution.py:14
  468.2 10.4 custom-call.66
  482.9 11.7 %cholesky.506 = f32[128,128]{1,0:T(8,128)S(1)} custom-call(f32[128,128]{1,0:T(8,128)S(1)} %cholesky.599), custom_call_target="Cholesky" | custom-call | tf_op jit(solution)/shard_map/jit(cholesky)/cholesky | solution.py:14
  495.9 10.0 custom-call.67
  509.2 11.7 %cholesky.526 = f32[128,128]{1,0:T(8,128)S(1)} custom-call(f32[128,128]{1,0:T(8,128)S(1)} %cholesky.604), custom_call_target="Cholesky" | custom-call | tf_op jit(solution)/shard_map/jit(cholesky)/cholesky | solution.py:14
  522.2 9.8 custom-call.68
  535.0 12.0 %cholesky.546 = f32[128,128]{1,0:T(8,128)S(1)} custom-call(f32[128,128]{1,0:T(8,128)S(1)} %cholesky.609), custom_call_target="Cholesky" | custom-call | tf_op jit(solution)/shard_map/jit(cholesky)/cholesky | solution.py:14
  548.4 9.8 custom-call.69
  560.9 11.7 %cholesky.564 = f32[128,128]{1,0:T(8,128)S(1)} custom-call(f32[128,128]{1,0:T(8,128)S(1)} %convolution_subtract_fusion.13), custom_call_target="Cholesky" | custom-call | tf_op jit(solution)/shard_map/jit(cholesky)/cholesky | solution.py:14
  579.5 4.9 select_select_fusion
  584.4 29.0 %while.1 = (s32[]{:T(128)}, f32[1024,1024]{1,0:T(8,128)}, s32[8,2]{0,1:T(2,128)S(1)}, f32[8,128,128]{2,1,0:T(8,128)}, s32[]{:T(128)}) while((s32[]{:T(128)}, f32[1024,1024]{1,0:T(8,128)}, s32[8,2]{0,1:T(2,128)S(1)}, f32[8,128,128]{2,1,0:T(8,128)}, s32[]{:T(128)}) %tuple.57), condition=%wide.while_cond, body=%wide.while_body.sunk | while | flops 2 | bytes 132205 | solution.py:15
  585.1 3.0 bitcast_dynamic-update-slice_fusion.2
  588.7 3.0 bitcast_dynamic-update-slice_fusion.2
  592.3 3.0 bitcast_dynamic-update-slice_fusion.2
  596.0 3.0 bitcast_dynamic-update-slice_fusion.2
  599.6 3.0 bitcast_dynamic-update-slice_fusion.2
  603.2 3.0 bitcast_dynamic-update-slice_fusion.2
  606.9 3.0 bitcast_dynamic-update-slice_fusion.2
  610.5 2.9 bitcast_dynamic-update-slice_fusion.2
  613.4 80.2 %custom-call.70 = f32[8,128,128]{1,2,0:T(8,128)} custom-call(f32[8,128,128]{2,1,0:T(8,128)} %get-tuple-element.10), custom_call_target="InvertDiagBlocksLowerTriangular" | custom-call | tf_op jit(solution)/shard_map/jit(_solve_triangular)/triangular_solve | solution.py:15
  702.0 2.4 convolution_subtract_fusion.8
  705.4 2.8 convolution_subtract_fusion.9
  709.7 3.2 convolution_subtract_fusion.4
  714.0 3.6 convolution_subtract_fusion.7
  718.8 4.3 convolution_subtract_fusion.3
  724.2 33.9 %all-gather.6.cloned.1.call-done = bf16[2048,1024]{0,1:T(8,128)(2,1)} async-done(((bf16[512,1024]{0,1:T(8,128)(2,1)}), bf16[2048,1024]{0,1:T(8,128)(2,1)}) %all-gather.6.cloned.1.call-update) | async-done | bytes 4194320 | tf_op jit(solution)/shard_map/all_gather | solution.py:39
  758.1 24.2 %convolution_convert_fusion = bf16[1024,4096]{1,0:T(8,128)(2,1)} fusion(bf16[2048,1024]{0,1:T(8,128)(2,1)} %all-gather.6.cloned.1.call-done, bf16[2048,4096]{1,0:T(8,128)(2,1)} %param.4, bf16[2048,4096]{1,0:T(8,128)(2,1)} %param.3), kind=kOutput, calls=%fused_computation.10 | convolution fusion | flops 17217617920 | bytes 46137344 | tf_op jit(solution)/shard_map/dot_general | solution.py:41
  782.3 147.5 %reduce-scatter.5.cloned.1.call-done = bf16[128,4096]{1,0:T(8,128)(2,1)} async-done(((bf16[1024,4096]{1,0:T(8,128)(2,1)}), bf16[128,4096]{1,0:T(8,128)(2,1)}) %reduce-scatter.5.cloned.1.call-update) | async-done | bytes 1048592 | tf_op jit(solution)/shard_map/reduce_scatter | solution.py:40
  929.9 125.6 %all-gather.8.cloned.1.call-done = bf16[1024,4096]{1,0:T(8,128)(2,1)} async-done(((bf16[128,4096]{1,0:T(8,128)(2,1)}), bf16[1024,4096]{1,0:T(8,128)(2,1)}) %all-gather.8.cloned.1.call-update) | async-done | bytes 8388624 | tf_op jit(solution)/shard_map/all_gather | solution.py:49
  1055.5 5.1 fusion
  1060.5 5.9 psum.15
  1066.5 26.4 %multiply_convert_fusion = bf16[2048,4096]{1,0:T(8,128)(2,1)} fusion(bf16[2048,1024]{0,1:T(8,128)(2,1)} %all-gather.6.cloned.1.call-done, bf16[1024,4096]{1,0:T(8,128)(2,1)} %all-gather.8.cloned.1.call-done, f32[1024]{0:T(1024)S(1)} %add_rsqrt_fusion), kind=kOutput, calls=%fused_computation.2 | convolution fusion | flops 17209229312 | bytes 29364224 | tf_op jit(solution)/shard_map/dot_general | solution.py:55
  1092.9 30.5 %subtract_convert_fusion = bf16[2048,4096]{1,0:T(8,128)(2,1)} fusion(bf16[2048,1024]{0,1:T(8,128)(2,1)S(1)} %copy-done.5, bf16[1024,4096]{1,0:T(8,128)(2,1)} %all-gather.8.cloned.1.call-done, bf16[2048,4096]{1,0:T(8,128)(2,1)} %param.4, bf16[2048,4096]{1,0:T(8,128)(2,1)} %param.3), kind=kOutput, calls=%fused_computation.3 | convolution fusion | flops 17246978048 | bytes 62914560 | tf_op jit(solution)/shard_map/dot_general | solution.py:54
  (99 shorter events, 59.9 us)
Async XLA Ops:
  7.2 130.2 %all-gather.4.cloned.1.call-start = ((), (), s32[]{:S(2)}) async-start(), calls=%async_computation.2 | async-start | bytes 9437184 | tf_op jit(solution)/shard_map/all_gather | solution.py:30
  7.9 198.2 %reduce-scatter.3.cloned.1.call-start = ((), (), s32[]{:S(2)}) async-start(), calls=%async_computation.3 | async-start | bytes 5242880 | tf_op jit(solution)/shard_map/reduce_scatter | solution.py:34
  163.1 191.4 %all-reduce.3.cloned.1.call-start = ((), (), s32[]{:S(2)}) async-start(), calls=%async_computation.4 | async-start | bytes 8388608 | tf_op jit(solution)/shard_map/psum | solution.py:37
  206.1 5.0 copy-start
  211.0 547.1 %all-gather.6.cloned.1.call-start = ((), (), s32[]{:S(2)}) async-start(), calls=%async_computation.5 | async-start | bytes 5242880 | tf_op jit(solution)/shard_map/all_gather | solution.py:39
  364.5 2.0 copy-start.1
  394.5 0.8 copy-start.3
  693.6 7.2 copy-start.4
  724.2 205.7 %reduce-scatter.5.cloned.1.call-start = ((), (), s32[]{:S(2)}) async-start(), calls=%async_computation.6 | async-start | bytes 9437184 | tf_op jit(solution)/shard_map/reduce_scatter | solution.py:40
  782.3 273.2 %all-gather.8.cloned.1.call-start = ((), (), s32[]{:S(2)}) async-start(), calls=%async_computation.7 | async-start | bytes 9437184 | tf_op jit(solution)/shard_map/all_gather | solution.py:49
  1066.5 26.4 %copy-start.5 = (bf16[2048,1024]{0,1:T(8,128)(2,1)S(1)}, bf16[2048,1024]{0,1:T(8,128)(2,1)}, u32[]{:S(2)}) copy-start(bf16[2048,1024]{0,1:T(8,128)(2,1)} %all-gather.6.cloned.1.call-done) | copy-start | bytes 12582916
  1092.9 30.5 %copy-start.2 = (bf16[128,4096]{1,0:T(8,128)(2,1)S(1)}, bf16[128,4096]{1,0:T(8,128)(2,1)}, u32[]{:S(2)}) copy-start(bf16[128,4096]{1,0:T(8,128)(2,1)} %reduce-scatter.5.cloned.1.call-done) | copy-start | bytes 3145732
Sparse Core Ops, SparseCore 0:
  10.1 127.1 all-gather.3
  163.3 42.7 reduce-scatter.2
  212.2 142.2 all-reduce.2
  724.3 33.7 all-gather.5
  782.4 147.4 reduce-scatter.4
  931.9 123.5 all-gather.7
where the time goes:
time: 1140 us; the launch traced here: 1130 us
  waiting for transfers between devices  623 us (55%)
  other arithmetic  275 us (24%)
  matrix products  167 us (15%)
  local copies, waits for them, and re-layouts  41.1 us (4%)
  between operations  19.9 us (2%)
    another operation x30, other arithmetic, orthonormalize(): lower_factor = jnp.linalg.cholesky(gram_matrix)  178 us
    reduce_scatter x1, waiting for transfers between devices, body(): lax.psum_scatter(lax.dot_general(orthonormal, buffer, (((0,), (0,)), ((),...  148 us
    psum x1, waiting for transfers between devices, body(): gram_matrix = lax.psum(self_gram(row_share), ('row', 'col'))  143 us
    all_gather x1, waiting for transfers between devices, body(): lax.all_gather(right_basis, 'row', axis=0, tiled=True)  129 us
    all_gather x1, waiting for transfers between devices, body(): gathered = lax.all_gather(right_share, 'row', axis=0, tiled=True)  126 us
    another operation x3, other arithmetic, orthonormalize(): jax.scipy.linalg.solve_triangular(lower_factor, projected.T, lower=True)  85.1 us
    reduce_scatter x1, waiting for transfers between devices, body(): lax.psum_scatter(partial_value.astype(jnp.bfloat16), 'col', scatter_dimen...  42.9 us
    all_gather x1, waiting for transfers between devices, body(): orthonormal = lax.all_gather(ortho_share, 'col', axis=0, tiled=True)  33.9 us
  transfers between devices with their start and end apart: 6, of which 6 were waited for; matrix products, arithmetic and copies ran while one was open for 0% of the time, Pallas kernels for 0%

commit v1 on v0

--- a/solution.py
+++ b/solution.py
@@ -8,6 +8,18 @@
 RANK = 1024
 momentum_decay = 0.95
 epsilon = 1e-06
+
+
+def gather_by_bits(x, axis, dim):
+    ways, here, turn = (lax.axis_size(axis), lax.axis_index(axis), x.shape[dim])
+    line, have = (x, 1)
+    while have < ways:
+        line = jnp.concatenate(
+            [line, lax.ppermute(line, axis, [(d, (d - have) % ways) for d in range(ways)])],
+            axis=dim,
+        )
+        have = 2 * have
+    return jnp.roll(line, here * turn, axis=dim)
 
 
 def orthonormalize(projected, gram_matrix):
@@ -27,7 +39,7 @@
     rank_rows = right_basis.shape[0]
     partial_value = lax.dot_general(
         buffer,
-        lax.all_gather(right_basis, "row", axis=0, tiled=True),
+        gather_by_bits(right_basis, "row", 0),
         (((1,), (1,)), ((), ())),
         preferred_element_type=jnp.float32,
     )

time: 1140 us -> 1290 us (1.13)
  waiting for transfers between devices: 623 us -> 741 us
  local copies, waits for them, and re-layouts: 41.1 us -> 58.8 us
    ppermute x0 -> x3, waiting for transfers between devices: none -> 244 us  [gather_by_bits(): lax.ppermute(line, axis, [(d, (d - have) % ways) for d in range(ways)])]
    all_gather x1 -> x0, waiting for transfers between devices: 129 us -> none  [body(): lax.all_gather(right_basis, 'row', axis=0, tiled=True)]
    unnamed x18 -> x31, local copies, waits for them, and re-layouts: 3.26 us -> 16.3 us
  transfers between devices with their start and end apart: 6 -> 8, of which waited for: 6 -> 8; matrix products, arithmetic and copies ran while one was open for 0% -> 0% of each run, Pallas kernels for 0% -> 0%
where the time goes in v1:
time: 1290 us; the launch traced here: 1280 us
  waiting for transfers between devices  741 us (57%)
  other arithmetic  279 us (22%)
  matrix products  167 us (13%)
  local copies, waits for them, and re-layouts  58.8 us (5%)
  between operations  19.6 us (2%)
    ppermute x3, waiting for transfers between devices, gather_by_bits(): lax.ppermute(line, axis, [(d, (d - have) % ways) for d in range(ways)])  244 us
    another operation x30, other arithmetic, orthonormalize(): lower_factor = jnp.linalg.cholesky(gram_matrix)  178 us
    reduce_scatter x1, waiting for transfers between devices, body(): lax.psum_scatter(lax.dot_general(orthonormal, buffer, (((0,), (0,)), ((),...  148 us
    psum x1, waiting for transfers between devices, body(): gram_matrix = lax.psum(self_gram(row_share), ('row', 'col'))  143 us
    all_gather x1, waiting for transfers between devices, body(): gathered = lax.all_gather(right_share, 'row', axis=0, tiled=True)  126 us
    another operation x3, other arithmetic, orthonormalize(): jax.scipy.linalg.solve_triangular(lower_factor, projected.T, lower=True)  85.1 us
    reduce_scatter x1, waiting for transfers between devices, body(): lax.psum_scatter(partial_value.astype(jnp.bfloat16), 'col', scatter_dimen...  46.5 us
    all_gather x1, waiting for transfers between devices, body(): orthonormal = lax.all_gather(ortho_share, 'col', axis=0, tiled=True)  33.9 us
  transfers between devices with their start and end apart: 8, of which 8 were waited for; matrix products, arithmetic and copies ran while one was open for 0% of the time, Pallas kernels for 0%

profile of v1, /device:TPU:0, one launch (start us, length us, event | category | flops | bytes accessed | tf_op | source)
XLA Modules:
  0.0 1279.6 jit_solution(16016995139956910277)
XLA Ops:
  7.2 6.1 collective-permute-start
  13.3 22.7 %collective-permute-done = bf16[128,4096]{1,0:T(8,128)(2,1)S(1)} collective-permute-done((bf16[128,4096]{1,0:T(8,128)(2,1)}, bf16[128,4096]{1,0:T(8,128)(2,1)S(1)}, u32[]{:S(2)}, u32[]{:S(2)}) %collective-permute-start) | collective-permute-done | bytes 1048608 | tf_op jit(solution)/shard_map/ppermute | solution.py:18
  39.3 45.1 %collective-permute-done.1 = bf16[256,4096]{1,0:T(8,128)(2,1)S(1)} collective-permute-done((bf16[256,4096]{1,0:T(8,128)(2,1)S(1)}, bf16[256,4096]{1,0:T(8,128)(2,1)S(1)}, u32[]{:S(2)}, u32[]{:S(2)}) %collective-permute-start.1) | collective-permute-done | bytes 2097184 | tf_op jit(solution)/shard_map/ppermute | solution.py:18
  91.8 176.5 %collective-permute-done.2 = bf16[512,4096]{1,0:T(8,128)(2,1)} collective-permute-done((bf16[512,4096]{1,0:T(8,128)(2,1)}, bf16[512,4096]{1,0:T(8,128)(2,1)}, u32[]{:S(2)}, u32[]{:S(2)}) %collective-permute-start.2) | collective-permute-done | bytes 4194336 | tf_op jit(solution)/shard_map/ppermute | solution.py:18
  268.3 4.7 constant_dynamic-update-slice_fusion.4
  276.5 4.7 constant_dynamic-update-slice_fusion
  281.2 25.8 %fusion.7 = bf16[2048,1024]{1,0:T(8,128)(2,1)} fusion(bf16[2048,4096]{1,0:T(8,128)(2,1)} %constant_dynamic-update-slice_fusion, s32[]{:T(128)S(6)} %select_n.21, bf16[2048,4096]{1,0:T(8,128)(2,1)} %param.4, bf16[2048,4096]{1,0:T(8,128)(2,1)} %param.3), kind=kOutput, calls=%fused_computation.18 | convolution fusion | flops 17215520768 | bytes 46137348 | tf_op jit(solution)/shard_map/dot_general | solution.py:40
  307.1 46.5 %reduce-scatter.3.cloned.1.call-done = bf16[512,1024]{1,0:T(8,128)(2,1)} async-done(((bf16[2048,1024]{1,0:T(8,128)(2,1)}), bf16[512,1024]{1,0:T(8,128)(2,1)}) %reduce-scatter.3.cloned.1.call-update) | async-done | bytes 1048592 | tf_op jit(solution)/shard_map/reduce_scatter | solution.py:46
  353.5 4.9 fusion.73
  358.8 143.2 %all-reduce.3.cloned.1.call-done = f32[1024,1024]{0,1:T(8,128)} async-done(((f32[1024,1024]{0,1:T(8,128)}), f32[1024,1024]{0,1:T(8,128)}) %all-reduce.3.cloned.1.call-update) | async-done | bytes 4194320 | tf_op jit(solution)/shard_map/psum | solution.py:49
  502.1 5.5 copy.7
  507.6 4.4 fusion.6
  514.1 11.7 cholesky.223
  525.8 9.8 custom-call.63
  542.8 12.1 cholesky.244
  555.5 9.8 custom-call.64
  570.3 13.2 %cholesky.468 = f32[128,128]{1,0:T(8,128)} custom-call(f32[128,128]{1,0:T(8,128)} %cholesky.589), custom_call_target="Cholesky" | custom-call | tf_op jit(solution)/shard_map/jit(cholesky)/cholesky | solution.py:26
  585.6 11.3 custom-call.65
  601.2 12.5 cholesky.487
  615.8 10.4 custom-call.66
  630.5 11.7 cholesky.506
  643.5 10.0 custom-call.67
  656.8 11.7 cholesky.526
  669.8 9.8 custom-call.68
  682.6 12.0 cholesky.546
  696.0 9.8 custom-call.69
  708.4 11.7 cholesky.564
  727.1 4.9 select_select_fusion
  732.0 29.0 %while.1 = (s32[]{:T(128)}, f32[1024,1024]{1,0:T(8,128)}, s32[8,2]{0,1:T(2,128)S(1)}, f32[8,128,128]{2,1,0:T(8,128)}, s32[]{:T(128)}) while((s32[]{:T(128)}, f32[1024,1024]{1,0:T(8,128)}, s32[8,2]{0,1:T(2,128)S(1)}, f32[8,128,128]{2,1,0:T(8,128)}, s32[]{:T(128)}) %tuple.57), condition=%wide.while_cond, body=%wide.while_body.sunk | while | flops 2 | bytes 132205 | solution.py:27
  732.6 3.0 bitcast_dynamic-update-slice_fusion.2
  736.3 3.0 bitcast_dynamic-update-slice_fusion.2
  739.9 3.0 bitcast_dynamic-update-slice_fusion.2
  743.6 3.0 bitcast_dynamic-update-slice_fusion.2
  747.2 3.0 bitcast_dynamic-update-slice_fusion.2
  750.8 3.0 bitcast_dynamic-update-slice_fusion.2
  754.5 3.0 bitcast_dynamic-update-slice_fusion.2
  761.0 80.2 %custom-call.70 = f32[8,128,128]{1,2,0:T(8,128)} custom-call(f32[8,128,128]{2,1,0:T(8,128)} %get-tuple-element.10), custom_call_target="InvertDiagBlocksLowerTriangular" | custom-call | tf_op jit(solution)/shard_map/jit(_solve_triangular)/triangular_solve | solution.py:27
  857.2 3.2 convolution_subtract_fusion.4
  861.6 3.6 convolution_subtract_fusion.7
  866.4 4.3 convolution_subtract_fusion.3
  871.8 33.9 %all-gather.3.cloned.1.call-done = bf16[2048,1024]{0,1:T(8,128)(2,1)} async-done(((bf16[512,1024]{0,1:T(8,128)(2,1)}), bf16[2048,1024]{0,1:T(8,128)(2,1)}) %all-gather.3.cloned.1.call-update) | async-done | bytes 4194320 | tf_op jit(solution)/shard_map/all_gather | solution.py:51
  905.7 24.2 %convolution_convert_fusion = bf16[1024,4096]{1,0:T(8,128)(2,1)} fusion(bf16[2048,1024]{0,1:T(8,128)(2,1)} %all-gather.3.cloned.1.call-done, bf16[2048,4096]{1,0:T(8,128)(2,1)} %param.4, bf16[2048,4096]{1,0:T(8,128)(2,1)} %param.3), kind=kOutput, calls=%fused_computation.12 | convolution fusion | flops 17217617920 | bytes 46137344 | tf_op jit(solution)/shard_map/dot_general | solution.py:53
  929.9 147.5 %reduce-scatter.5.cloned.1.call-done = bf16[128,4096]{1,0:T(8,128)(2,1)} async-done(((bf16[1024,4096]{1,0:T(8,128)(2,1)}), bf16[128,4096]{1,0:T(8,128)(2,1)}) %reduce-scatter.5.cloned.1.call-update) | async-done | bytes 1048592 | tf_op jit(solution)/shard_map/reduce_scatter | solution.py:52
  1077.5 125.6 %all-gather.5.cloned.1.call-done = bf16[1024,4096]{1,0:T(8,128)(2,1)} async-done(((bf16[128,4096]{1,0:T(8,128)(2,1)}), bf16[1024,4096]{1,0:T(8,128)(2,1)}) %all-gather.5.cloned.1.call-update) | async-done | bytes 8388624 | tf_op jit(solution)/shard_map/all_gather | solution.py:61
  1203.1 5.1 fusion
  1208.1 5.9 psum.15
  1214.1 26.4 %multiply_convert_fusion = bf16[2048,4096]{1,0:T(8,128)(2,1)} fusion(bf16[2048,1024]{0,1:T(8,128)(2,1)} %all-gather.3.cloned.1.call-done, bf16[1024,4096]{1,0:T(8,128)(2,1)} %all-gather.5.cloned.1.call-done, f32[1024]{0:T(1024)S(1)} %add_rsqrt_fusion), kind=kOutput, calls=%fused_computation.2 | convolution fusion | flops 17209229312 | bytes 29364224 | tf_op jit(solution)/shard_map/dot_general | solution.py:67
  1240.5 30.5 %subtract_convert_fusion = bf16[2048,4096]{1,0:T(8,128)(2,1)} fusion(bf16[2048,1024]{0,1:T(8,128)(2,1)S(1)} %copy-done.8, bf16[1024,4096]{1,0:T(8,128)(2,1)} %all-gather.5.cloned.1.call-done, bf16[2048,4096]{1,0:T(8,128)(2,1)} %param.4, bf16[2048,4096]{1,0:T(8,128)(2,1)} %param.3), kind=kOutput, calls=%fused_computation.3 | convolution fusion | flops 17246978048 | bytes 62914560 | tf_op jit(solution)/shard_map/dot_general | solution.py:66
  (118 shorter events, 86.4 us)
Async XLA Ops:
  7.2 77.2 %copy-start = (bf16[128,4096]{1,0:T(8,128)(2,1)S(1)}, bf16[128,4096]{1,0:T(8,128)(2,1)}, u32[]{:S(2)}) copy-start(bf16[128,4096]{1,0:T(8,128)(2,1)} %param.5) | copy-start | bytes 3145732
  7.2 346.4 %reduce-scatter.3.cloned.1.call-start = ((), (), s32[]{:S(2)}) async-start(), calls=%async_computation.2 | async-start | bytes 5242880 | tf_op jit(solution)/shard_map/reduce_scatter | solution.py:46
  7.2 28.8 %collective-permute-start = (bf16[128,4096]{1,0:T(8,128)(2,1)}, bf16[128,4096]{1,0:T(8,128)(2,1)S(1)}, u32[]{:S(2)}, u32[]{:S(2)}) collective-permute-start(bf16[128,4096]{1,0:T(8,128)(2,1)} %param.5), channel_id=1, source_target_pairs={{0,28},{4,0},{8,4},{12,8},{16,12},{20,16},{24,20},{28,24},{1,29},{... | collective-permute-start | bytes 3145736 | tf_op jit(solution)/shard_map/ppermute | solution.py:18
  36.0 50.6 %copy-start.1 = (bf16[128,4096]{1,0:T(8,128)(2,1)}, bf16[128,4096]{1,0:T(8,128)(2,1)S(1)}, u32[]{:S(2)}) copy-start(bf16[128,4096]{1,0:T(8,128)(2,1)S(1)} %collective-permute-done) | copy-start | bytes 3145732
  37.8 46.6 %collective-permute-start.1 = (bf16[256,4096]{1,0:T(8,128)(2,1)S(1)}, bf16[256,4096]{1,0:T(8,128)(2,1)S(1)}, u32[]{:S(2)}, u32[]{:S(2)}) collective-permute-start(bf16[256,4096]{1,0:T(8,128)(2,1)S(1)} %pad_maximum_fusion.1), channel_id=1, source_target_pairs={{0,24},{4,28},{8,0},{12,4},{16,8},{20,12},{24,16},{28,20},{1,25},{... | collective-permute-start | bytes 6291464 | tf_op jit(solution)/shard_map/ppermute | solution.py:18
  86.6 181.7 %collective-permute-start.2 = (bf16[512,4096]{1,0:T(8,128)(2,1)}, bf16[512,4096]{1,0:T(8,128)(2,1)}, u32[]{:S(2)}, u32[]{:S(2)}) collective-permute-start(bf16[512,4096]{1,0:T(8,128)(2,1)} %pad_maximum_fusion), channel_id=1, source_target_pairs={{0,16},{4,20},{8,24},{12,28},{16,0},{20,4},{24,8},{28,12},{1,17},{... | collective-permute-start | bytes 12582920 | tf_op jit(solution)/shard_map/ppermute | solution.py:18
  91.8 182.2 %copy-start.2 = (bf16[128,4096]{1,0:T(8,128)(2,1)S(1)}, bf16[128,4096]{1,0:T(8,128)(2,1)}, u32[]{:S(2)}) copy-start(bf16[128,4096]{1,0:T(8,128)(2,1)} %copy-done.1) | copy-start | bytes 3145732
  307.0 195.1 %all-reduce.3.cloned.1.call-start = ((), (), s32[]{:S(2)}) async-start(), calls=%async_computation.3 | async-start | bytes 8388608 | tf_op jit(solution)/shard_map/psum | solution.py:49
  353.5 5.0 copy-start.3
  358.5 547.2 %all-gather.3.cloned.1.call-start = ((), (), s32[]{:S(2)}) async-start(), calls=%async_computation.4 | async-start | bytes 5242880 | tf_op jit(solution)/shard_map/all_gather | solution.py:51
  512.1 2.0 copy-start.4
  542.0 0.8 copy-start.6
  841.2 7.2 copy-start.7
  871.8 205.7 %reduce-scatter.5.cloned.1.call-start = ((), (), s32[]{:S(2)}) async-start(), calls=%async_computation.5 | async-start | bytes 9437184 | tf_op jit(solution)/shard_map/reduce_scatter | solution.py:52
  929.9 273.2 %all-gather.5.cloned.1.call-start = ((), (), s32[]{:S(2)}) async-start(), calls=%async_computation.6 | async-start | bytes 9437184 | tf_op jit(solution)/shard_map/all_gather | solution.py:61
  1214.1 26.4 %copy-start.8 = (bf16[2048,1024]{0,1:T(8,128)(2,1)S(1)}, bf16[2048,1024]{0,1:T(8,128)(2,1)}, u32[]{:S(2)}) copy-start(bf16[2048,1024]{0,1:T(8,128)(2,1)} %all-gather.3.cloned.1.call-done) | copy-start | bytes 12582916
  1240.5 30.5 %copy-start.5 = (bf16[128,4096]{1,0:T(8,128)(2,1)S(1)}, bf16[128,4096]{1,0:T(8,128)(2,1)}, u32[]{:S(2)}) copy-start(bf16[128,4096]{1,0:T(8,128)(2,1)} %reduce-scatter.5.cloned.1.call-done) | copy-start | bytes 3145732
Sparse Core Ops, SparseCore 0:
  307.1 46.3 reduce-scatter.2
  359.7 142.3 all-reduce.2
  871.9 33.7 all-gather.2
  930.0 147.4 reduce-scatter.4
  1079.4 123.5 all-gather.4
